TPU v7x, 32 devices: a whole 2x2x4 slice. The times are simulated.
32 devices in a mesh: grp: 2 (over x), seq: 8 (over z, y), pool: 2 (over core).
Axes of the slice: x: 2, y: 2, z: 4, core: 2. Of those that a mesh axis runs over, the one named last changes fastest.
Arguments:
- factors: bfloat16 [2, 65536, 160], P('grp', 'seq'), parts along dimension 0, may hold values from -6 to 6
- basis: bfloat16 [2, 160, 1024], P('grp', None, 'pool'), parts along dimension 0, may hold values from -1 to 1
- value_pool: bfloat16 [2, 65536, 1024], P('grp', ('seq', 'pool')), parts along dimension 0, may hold values from -6 to 6
- page_summary: bfloat16 [2, 8192, 1024], P('grp', 'seq', 'pool'), parts along dimension 0, may hold values from -6 to 6
- recent_keys: bfloat16 [2, 64, 1024], P('grp', None, 'pool'), parts along dimension 0, may hold values from -20 to 20
- recent_values: bfloat16 [2, 64, 1024], P('grp', None, 'pool'), parts along dimension 0, may hold values from -6 to 6
- query: bfloat16 [2, 8192], P('grp', 'pool'), parts along dimension 0, may hold values from -8192 to 8192
- selected: int32 [2, 8, 1024], P('grp'), parts along dimension 0, may hold values from 0 to 8191, as said below
- owner_map: int32 [2, 8192], P('grp', 'seq'), parts along dimension 0, may hold values from 0 to 1, as said below
- lengths: int32 [2], P('grp'), parts along dimension 0, may hold values from 32768 to 65536, as said below
Outputs:
- attn: bfloat16 [2, 8192], P('grp', 'pool'), parts along dimension 0
There are 2 independent parts, one for each index of `grp`. A program takes and returns all parts, laid end to end along the dimension named above; each array names one. Nothing has to cross between parts.
Inputs may be any that keep to these rules, and one draw needn't show every extreme that they name: `selected`: for every request and key-value head, 1024 distinct page ids in ascending order, each below ceil(lengths / 8); every aligned block of 1024 pages holds at most 256 of them, and for every request and head some block holds exactly 256. `owner_map`: in every aligned block of 1024 pages of a request exactly half of the pages have owner 1. `lengths`: some request has exactly 65536 tokens.
All inputs are finite; a program needn't handle non-finite values.
Results may differ from a plain program's by a relative error of at most 0.0075.
The roundings to bfloat16 on the way count: a program that leaves them out, or rounds other values in their place, can miss the bound.
Values may be sent and summed in bfloat16 or wider, within the bound.
A program may use at most 128 MiB of HBM per device.

v0:
```python
import math
import jax
import jax.numpy as jnp
import numpy as np
from jax import lax
from jax.sharding import PartitionSpec as P

HD = 128
PAGE = 8
SEL = 1024
CAPMIN = 64
WIN = 64


def partner(x, axis, apart):
    return lax.ppermute(x, axis, [(i, i ^ 1 << apart) for i in range(lax.axis_size(axis))])


def llama_rates(head_dim):
    half_dim = head_dim // 2
    base_rates = 500000.0 ** (-(np.arange(half_dim) * 2.0) / head_dim)
    wavelen = 2.0 * math.pi / base_rates
    smooth = (8192.0 / wavelen - 1.0) / 3.0
    blended = (1.0 - smooth) * base_rates / 8.0 + smooth * base_rates
    return np.where(
        wavelen < 2048.0, base_rates, np.where(wavelen > 8192.0, base_rates / 8.0, blended)
    )


def angle_tables(length, head_dim):
    inv_rates = llama_rates(head_dim)
    coarse = (np.arange(length // 256) * 256.0)[:, None] * inv_rates[None, :]
    fine_angles = (np.arange(256) * 1.0)[:, None] * inv_rates[None, :]
    return (np.cos(coarse), np.sin(coarse), np.cos(fine_angles), np.sin(fine_angles))


def combine_angles(coarse_cos, coarse_sin, fine_cos, fine_sin):
    cosine = (
        coarse_cos[:, None, :] * fine_cos[None, :, :]
        - coarse_sin[:, None, :] * fine_sin[None, :, :]
    )
    sine_table = (
        coarse_sin[:, None, :] * fine_cos[None, :, :]
        + coarse_cos[:, None, :] * fine_sin[None, :, :]
    )
    row_count = coarse_cos.shape[0] * 256
    return (cosine.reshape(row_count, -1), sine_table.reshape(row_count, -1))


def rotate(values, cosine, sine_table):
    half_dim = values.shape[-1] // 2
    first_half = values[..., :half_dim]
    second_half = values[..., half_dim:]
    return jnp.concatenate(
        [
            first_half * cosine - second_half * sine_table,
            second_half * cosine + first_half * sine_table,
        ],
        axis=-1,
    )


def slot_pages(chosen_ids, first_page, pages_dev, capacity):
    before = jnp.sum((chosen_ids < first_page).astype(jnp.int32), axis=-1)
    inside = jnp.sum(
        ((chosen_ids >= first_page) & (chosen_ids < first_page + pages_dev)).astype(jnp.int32),
        axis=-1,
    )
    filler = jnp.zeros(chosen_ids.shape[:-1] + (capacity,), jnp.int32) + first_page
    padded = jnp.concatenate([chosen_ids, filler], axis=-1)
    offsets = before[..., None] + jnp.arange(capacity, dtype=jnp.int32)
    picked = jnp.take_along_axis(padded, offsets, axis=-1)
    slot_live = jnp.arange(capacity, dtype=jnp.int32) < inside[..., None]
    return (jnp.where(slot_live, picked - first_page, 0), slot_live)


def merge_parts(earlier, following):
    peak_a, sum_a, out_a = earlier
    peak_b, sum_b, out_b = following
    joint_peak = jnp.maximum(peak_a, peak_b)
    factor_a = jnp.exp(peak_a - joint_peak)
    factor_b = jnp.exp(peak_b - joint_peak)
    return (
        joint_peak,
        sum_a * factor_a + sum_b * factor_b,
        out_a * factor_a[..., None] + out_b * factor_b[..., None],
    )


def local(
    factors,
    basis,
    value_pool,
    page_summary,
    recent_keys,
    recent_values,
    query,
    selected,
    owner_map,
    lengths,
):
    requests, span_rows, rank_dim = factors.shape
    seq_count = lax.axis_size("seq")
    seq_pos = lax.axis_index("seq")
    core_index = lax.axis_index("pool")
    heads_here = basis.shape[2] // HD
    group_size = query.shape[1] // (heads_here * HD)
    pages_dev = span_rows // PAGE
    half_pages = pages_dev // 2
    capacity = max(CAPMIN, 2 * SEL // seq_count)
    score_scale = HD ** (-0.5)
    first_token = seq_pos * span_rows
    first_page = seq_pos * pages_dev
    tables = angle_tables(span_rows * seq_count, HD)
    blocks = span_rows // 256
    coarse_cos = lax.dynamic_slice_in_dim(
        jnp.asarray(tables[0], jnp.float32), seq_pos * blocks, blocks, 0
    )
    coarse_sin = lax.dynamic_slice_in_dim(
        jnp.asarray(tables[1], jnp.float32), seq_pos * blocks, blocks, 0
    )
    cosine, sine_table = combine_angles(
        coarse_cos,
        coarse_sin,
        jnp.asarray(tables[2], jnp.float32),
        jnp.asarray(tables[3], jnp.float32),
    )
    stacked = jnp.einsum("rtk,rkc->rtc", factors, basis, preferred_element_type=jnp.float32)
    stacked = stacked.reshape(requests, span_rows, heads_here, HD)
    keys_bf = rotate(stacked, cosine[None, :, None, :], sine_table[None, :, None, :]).astype(
        jnp.bfloat16
    )
    positions = first_token + jnp.arange(span_rows, dtype=jnp.int32)
    in_range = positions[None, :] < lengths[:, None]
    page_valid = in_range.reshape(requests, pages_dev, PAGE)
    any_valid = jnp.any(page_valid, axis=2)
    paged_keys = keys_bf.reshape(requests, pages_dev, PAGE, heads_here, HD)
    token_mask = page_valid[:, :, :, None, None]
    low_keys = jnp.min(jnp.where(token_mask, paged_keys, jnp.inf), axis=2)
    high_keys = jnp.max(jnp.where(token_mask, paged_keys, -jnp.inf), axis=2)
    center = jnp.where(
        any_valid[:, :, None, None],
        (low_keys.astype(jnp.float32) + high_keys.astype(jnp.float32)) * 0.5,
        0.0,
    ).astype(jnp.bfloat16)
    queries = query.reshape(requests, heads_here, group_size, HD)
    request_idx = jnp.arange(requests, dtype=jnp.int32)[:, None, None]
    local_heads = jnp.arange(heads_here, dtype=jnp.int32)
    my_heads = (core_index * heads_here + local_heads)[None, :, None]
    other_heads = ((1 - core_index) * heads_here + local_heads)[None, :, None]
    ones_count = jnp.cumsum(owner_map, axis=1)
    zeros_count = jnp.cumsum(1 - owner_map, axis=1)
    page_rank = jnp.where(owner_map == 1, ones_count, zeros_count) - 1
    my_ids = lax.dynamic_slice_in_dim(selected, core_index * heads_here, heads_here, 1)
    other_ids = lax.dynamic_slice_in_dim(selected, (1 - core_index) * heads_here, heads_here, 1)
    my_local, my_live = slot_pages(my_ids, first_page, pages_dev, capacity)
    other_local, other_live = slot_pages(other_ids, first_page, pages_dev, capacity)
    my_owner = owner_map[request_idx, my_local]
    my_rank = page_rank[request_idx, my_local]
    other_owner = owner_map[request_idx, other_local]
    other_rank = page_rank[request_idx, other_local]
    held_here = my_owner == core_index
    other_held = (other_owner == core_index) & other_live
    key_rows = paged_keys[request_idx, my_local, :, local_heads[None, :, None], :]
    exact_scores = (
        jnp.einsum("rhgd,rhcpd->rhgcp", queries, key_rows, preferred_element_type=jnp.float32)
        * score_scale
    )
    token_pos = first_token + my_local[..., None] * PAGE + jnp.arange(PAGE, dtype=jnp.int32)
    exact_ok = my_live[..., None] & (token_pos < lengths[:, None, None, None])
    exact_scores = jnp.where(exact_ok[:, :, None], exact_scores, -jnp.inf)
    chosen_mask = jnp.any(
        (my_local[..., None] == jnp.arange(pages_dev, dtype=jnp.int32)) & my_live[..., None], axis=2
    )
    land_scores = (
        jnp.einsum("rhgd,rphd->rhgp", queries, center, preferred_element_type=jnp.float32)
        * score_scale
    )
    land_ok = any_valid[:, None, :] & jnp.logical_not(chosen_mask)
    land_scores = jnp.where(land_ok[:, :, None, :], land_scores, -jnp.inf)
    row_peak = jnp.maximum(
        jnp.maximum(jnp.max(exact_scores, axis=(3, 4)), jnp.max(land_scores, axis=3)), -1e30
    )
    exact_w = jnp.exp(exact_scores - row_peak[..., None, None])
    land_w = jnp.exp(land_scores - row_peak[..., None])
    weight_sum = jnp.sum(exact_w, axis=(3, 4)) + jnp.sum(land_w, axis=3)
    exact_b = exact_w.astype(jnp.bfloat16)
    land_b = land_w.astype(jnp.bfloat16)
    summary = page_summary.reshape(requests, pages_dev, heads_here, HD)
    partial_value = jnp.einsum(
        "rhgp,rphd->rhgd", land_b, summary, preferred_element_type=jnp.float32
    )
    value_store = value_pool.reshape(requests, half_pages, PAGE, value_pool.shape[2] // HD, HD)
    local_rows = value_store[request_idx, my_rank, :, my_heads, :]
    outgoing_rows = value_store[request_idx, other_rank, :, other_heads, :]
    outgoing = jnp.where(other_held[..., None, None], outgoing_rows, jnp.zeros_like(outgoing_rows))
    incoming = partner(outgoing, "pool", 0)
    value_rows = jnp.where(held_here[..., None, None], local_rows, incoming)
    partial_value = partial_value + jnp.einsum(
        "rhgcp,rhcpd->rhgd", exact_b, value_rows, preferred_element_type=jnp.float32
    )
    recent_k = recent_keys.reshape(requests, WIN, heads_here, HD)
    recent_v = recent_values.reshape(requests, WIN, heads_here, HD)
    recent_scores = (
        jnp.einsum("rhgd,rwhd->rhgw", queries, recent_k, preferred_element_type=jnp.float32)
        * score_scale
    )
    recent_peak = jnp.max(recent_scores, axis=3)
    recent_w = jnp.exp(recent_scores - recent_peak[..., None])
    recent_sum = jnp.sum(recent_w, axis=3)
    recent_out = jnp.einsum(
        "rhgw,rwhd->rhgd",
        recent_w.astype(jnp.bfloat16),
        recent_v,
        preferred_element_type=jnp.float32,
    )
    row_total = requests * heads_here * group_size
    row_share = row_total // seq_count
    got_peak, got_sum, got_out = (
        lax.all_to_all(
            row_peak.reshape(1, row_total), "seq", split_axis=1, concat_axis=0, tiled=True
        ),
        lax.all_to_all(
            weight_sum.reshape(1, row_total), "seq", split_axis=1, concat_axis=0, tiled=True
        ),
        lax.all_to_all(
            partial_value.reshape(1, row_total, HD), "seq", split_axis=1, concat_axis=0, tiled=True
        ),
    )
    joint_peak = jnp.max(got_peak, axis=0)
    factor = jnp.exp(got_peak - joint_peak[None, :])
    summed = jnp.sum(got_sum * factor, axis=0)
    gathered_out = jnp.sum(got_out * factor[..., None], axis=0)
    row_start = seq_pos * row_share
    mine_peak = lax.dynamic_slice_in_dim(recent_peak.reshape(row_total), row_start, row_share, 0)
    mine_sum = lax.dynamic_slice_in_dim(recent_sum.reshape(row_total), row_start, row_share, 0)
    mine_out = lax.dynamic_slice_in_dim(recent_out.reshape(row_total, HD), row_start, row_share, 0)
    final_peak, final_sum, final_out = merge_parts(
        (joint_peak, summed, gathered_out), (mine_peak, mine_sum, mine_out)
    )
    rows_out = (final_out / final_sum[:, None]).astype(jnp.bfloat16)
    all_rows = lax.all_gather(rows_out, "seq", axis=0, tiled=True)
    return all_rows.reshape(requests, heads_here * group_size * HD)


def solution(mesh):
    placed = (
        P("grp", "seq", None),
        P("grp", None, "pool"),
        P("grp", ("seq", "pool"), None),
        P("grp", "seq", "pool"),
        P("grp", None, "pool"),
        P("grp", None, "pool"),
        P("grp", "pool"),
        P("grp", None, None),
        P("grp", "seq"),
        P("grp"),
    )
    return jax.shard_map(
        local, mesh=mesh, in_specs=placed, out_specs=P("grp", "pool"), check_vma=False
    )
```

profile of v0, /device:TPU:0, one launch (start us, length us, event | category | flops | bytes accessed | tf_op | source)
XLA Modules:
  0.0 208.9 jit_solution(5469197252403658698)
XLA Ops:
  1.2 9.1 %gather_fusion.7 = s32[1024]{0:T(1024)S(1)} fusion(s32[4,1280]{1,0:T(4,128)S(1)} %get-tuple-element.43, s32[1024]{0:T(1024)S(1)} %bitcast.168), kind=kCustom, calls=%fused_computation.clone | custom fusion | bytes 16384 | tf_op jit(solution)/shard_map/jit(take_along_axis)/gather | solution.py:72
  11.9 9.1 %gather_fusion.8 = s32[1024]{0:T(1024)S(1)} fusion(s32[4,1280]{1,0:T(4,128)S(1)} %get-tuple-element.42, s32[1024]{0:T(1024)S(1)} %bitcast.169), kind=kCustom, calls=%fused_computation.1.clone | custom fusion | bytes 16384 | tf_op jit(solution)/shard_map/jit(take_along_axis)/gather | solution.py:72
  21.1 6.5 %gather_fusion.4 = s32[1024]{0:T(1024)S(1)} fusion(s32[1,1024]{1,0:T(1,128)S(1)} %copy-done.2, s32[1024]{0:T(1024)S(1)} %bitcast.163), kind=kCustom, calls=%fused_computation.6 | custom fusion | bytes 16384 | tf_op jit(solution)/shard_map/gather | solution.py:160
  27.7 6.5 %gather_fusion.5 = s32[1024]{0:T(1024)S(1)} fusion(s32[1,1024]{1,0:T(1,128)S(1)} %fusion.47, s32[1024]{0:T(1024)S(1)} %bitcast.164), kind=kCustom, calls=%fused_computation.7 | custom fusion | bytes 16384 | tf_op jit(solution)/shard_map/gather | solution.py:161
  34.2 6.5 %gather_fusion.2 = s32[1024]{0:T(1024)S(1)} fusion(s32[1,1024]{1,0:T(1,128)S(1)} %fusion.47, s32[1024]{0:T(1024)S(1)} %bitcast.161), kind=kCustom, calls=%fused_computation.4 | custom fusion | bytes 16384 | tf_op jit(solution)/shard_map/gather | solution.py:159
  41.0 12.5 %gather_fusion.6 = bf16[1024,8,128]{2,1,0:T(8,128)(2,1)} fusion(bf16[1,512,8,8,128]{4,2,3,1,0:T(8,128)(2,1)} %bitcast.178, s32[1024]{0:T(1024)S(1)} %bitcast.166), kind=kCustom, calls=%fused_computation.8 | custom fusion | bytes 4206592 | tf_op jit(solution)/shard_map/gather | solution.py:195
  53.5 4.5 %broadcast_select_fusion = bf16[1,4,256,8,128]{4,3,2,1,0:T(8,128)(2,1)} fusion(bf16[1,4,256,8,128]{4,3,2,1,0:T(8,128)(2,1)} %bitcast.174, pred[4,256]{1,0:T(4,128)(4,1)S(1)} %fusion.84), kind=kLoop, calls=%fused_computation.26 | loop fusion | flops 1048576 | bytes 4195328 | tf_op jit(solution)/shard_map/jit(_where)/select_n | solution.py:196
  66.7 5.9 %subtract_convert_fusion = (bf16[1,8192,4,64]{1,3,2,0:T(8,128)(2,1)}, bf16[1,8192,4,64]{1,3,2,0:T(8,128)(2,1)}) fusion(f32[1,8192,4,128]{1,3,2,0:T(8,128)S(1)} %convolution_bitcast_fusion, f32[8192,64]{0,1:T(8,128)} %bitcast.173, f32[8192,64]{0,1:T(8,128)} %bitcast.172), kind=kLoop, calls=%fused_computation.14 | loop fusion | flops 16777216 | bytes 29360128 | tf_op jit(solution)/shard_map/convert.3
  72.6 8.4 %copy.71 = bf16[1,8192,4,64]{3,1,2,0:T(8,128)(2,1)} copy(bf16[1,8192,4,64]{1,3,2,0:T(8,128)(2,1)} %get-tuple-element.22) | data formatting | bytes 8388608 | tf_op jit(solution)/shard_map/convert.2
  81.0 8.5 %copy.70 = bf16[1,8192,4,64]{3,1,2,0:T(8,128)(2,1)} copy(bf16[1,8192,4,64]{1,3,2,0:T(8,128)(2,1)} %get-tuple-element.21) | data formatting | bytes 8388608 | tf_op jit(solution)/shard_map/convert.3
  91.3 22.4 %select_reduce_fusion.1 = (bf16[1024,4,128]{2,1,0:T(4,128)(2,1)S(1)}, bf16[1024,4,128]{2,1,0:T(4,128)(2,1)S(1)}, bf16[1,1024,8,4,128]{4,2,3,1,0:T(8,128)(2,1)}) fusion(pred[1024,8]{1,0:T(8,128)(4,1)S(1)} %copy.68, bf16[1,1024,8,4,64]{4,2,1,3,0:T(8,128)(2,1)} %bitcast.170, bf16[1,1024,8,4,64]{4,2,1,3,0:T(8,128)(2,1)} %bitcast.171), kind=kLoop, calls=%fused_computation.12 | loop fusion | flops 32505856 | bytes 18882560 | tf_op jit(solution)/shard_map/reduce_min | solution.py:139
  113.7 4.5 %select_convert_fusion = bf16[1024,4,128]{2,1,0:T(4,128)(2,1)} fusion(bf16[1024,4,128]{2,1,0:T(4,128)(2,1)S(1)} %get-tuple-element.7, bf16[1024,4,128]{2,1,0:T(4,128)(2,1)S(1)} %get-tuple-element.6, pred[1024]{0:T(1024)(128)(4,1)S(1)} %fusion.29), kind=kLoop, calls=%fused_computation.22 | loop fusion | flops 3145728 | bytes 3146752 | tf_op jit(solution)/shard_map/convert_element_type | solution.py:145
  118.3 7.6 %gather_fusion = bf16[1024,8,128]{2,1,0:T(8,128)(2,1)S(1)} fusion(bf16[1,1024,8,4,128]{4,2,3,1,0:T(8,128)(2,1)} %get-tuple-element.23, s32[1024]{0:T(1024)S(1)} %bitcast.165), kind=kCustom, calls=%fused_computation.2 | custom fusion | bytes 4206592 | tf_op jit(solution)/shard_map/gather | solution.py:164
  126.0 2.6 %fusion.40 = f32[4,256,8,8]{3,2,1,0:T(8,128)} fusion(bf16[4,256,8,128]{3,2,1,0:T(8,128)(2,1)S(1)} %bitcast.177, bf16[4096]{0:T(1024)(128)(2,1)S(1)} %reduce.21), kind=kOutput, calls=%fused_computation.83 | convolution fusion | flops 16777216 | bytes 2367488 | tf_op jit(solution)/shard_map/rhgd,rhcpd->rhgcp/dot_general | solution.py:166
  129.1 2.8 %copy.75 = f32[4,256,8,8]{1,2,3,0:T(8,128)S(1)} copy(f32[4,256,8,8]{3,2,1,0:T(8,128)} %fusion.40) | data formatting | bytes 524288 | tf_op jit(solution)/shard_map/rhgd,rhcpd->rhgcp/dot_general | solution.py:166
  133.2 6.8 %all-to-all-start.2 = ((f32[1,8,4]{2,0,1:T(1,128)}), f32[1,8,4]{2,0,1:T(1,128)S(1)}, u32[]{:S(2)}, u32[]{:S(2)}) async-start(f32[1,8,4]{2,0,1:T(1,128)} %bitcast.44), calls=%async_computation.2 | async-start | bytes 8192 | tf_op jit(solution)/shard_map/all_to_all | solution.py:223
  140.0 6.5 %gather_fusion.1 = s32[1024]{0:T(1024)S(1)} fusion(s32[1,1024]{1,0:T(1,128)S(1)} %copy-done.2, s32[1024]{0:T(1024)S(1)} %bitcast.162), kind=kCustom, calls=%fused_computation.3 | custom fusion | bytes 16384 | tf_op jit(solution)/shard_map/gather | solution.py:158
  150.6 12.5 %gather_fusion.3 = bf16[1024,8,128]{2,1,0:T(8,128)(2,1)} fusion(bf16[1,512,8,8,128]{4,2,3,1,0:T(8,128)(2,1)} %bitcast.179, s32[1024]{0:T(1024)S(1)} %bitcast.167), kind=kCustom, calls=%fused_computation.5 | custom fusion | bytes 4206592 | tf_op jit(solution)/shard_map/gather | solution.py:194
  163.1 6.0 %all-to-all-start.1 = ((f32[1,8,4]{2,0,1:T(1,128)}), f32[1,8,4]{2,0,1:T(1,128)S(1)}, u32[]{:S(2)}, u32[]{:S(2)}) async-start(f32[1,8,4]{2,0,1:T(1,128)} %bitcast.41), calls=%async_computation.1 | async-start | bytes 8192 | tf_op jit(solution)/shard_map/all_to_all | solution.py:220
  169.3 6.3 %all-to-all-done.1 = f32[1,8,4]{2,0,1:T(1,128)S(1)} async-done(((f32[1,8,4]{2,0,1:T(1,128)}), f32[1,8,4]{2,0,1:T(1,128)S(1)}, u32[]{:S(2)}, u32[]{:S(2)}) %all-to-all-start.1) | async-done | bytes 160 | tf_op jit(solution)/shard_map/all_to_all | solution.py:220
  175.9 5.5 %fusion.12 = f32[4,8,128]{2,1,0:T(8,128)} fusion(f32[4,8,128]{2,1,0:T(8,128)S(1)} %fusion.15, bf16[4,8,256,8]{3,1,2,0:T(8,128)(2,1)} %copy.77, bf16[1,4,256,8,128]{4,3,2,1,0:T(8,128)(2,1)} %bitcast.180, bf16[1,4,256,8,128]{4,3,2,1,0:T(8,128)(2,1)} %collective-permute-done, pred[4,256]{1,0:T(4,128)(4,1)S(1)} %reshape.1025), kind=kOutput, calls=%fused_computation.33 | convolution fusion | flops 17829888 | bytes 4359168 | tf_op jit(solution)/shard_map/rhgcp,rhcpd->rhgd/dot_general | solution.py:199
  181.4 3.3 %all-to-all-start = ((f32[1,32,128]{2,0,1:T(1,128)}), f32[1,32,128]{2,0,1:T(1,128)S(1)}, u32[]{:S(2)}, u32[]{:S(2)}) async-start(f32[1,32,128]{2,0,1:T(1,128)} %bitcast.39), calls=%async_computation | async-start | bytes 32768 | tf_op jit(solution)/shard_map/all_to_all | solution.py:226
  184.9 6.3 %all-to-all-done = f32[1,32,128]{2,0,1:T(1,128)S(1)} async-done(((f32[1,32,128]{2,0,1:T(1,128)}), f32[1,32,128]{2,0,1:T(1,128)S(1)}, u32[]{:S(2)}, u32[]{:S(2)}) %all-to-all-start) | async-done | bytes 16416 | tf_op jit(solution)/shard_map/all_to_all | solution.py:226
  191.4 16.9 %all-gather = bf16[8,4,128]{2,1,0:T(4,128)(2,1)S(1)} all-gather(bf16[1,4,128]{2,1,0:T(4,128)(2,1)S(1)} %fusion.88), channel_id=1, replica_groups=mesh['grp'=2,'seq'=8,'pool'=2] {'seq'}, dimensions={0}, use_global_device_ids=true | all-gather | bytes 9216 | tf_op jit(solution)/shard_map/all_gather | solution.py:242
  (118 shorter events, 20.4 us)
Async XLA Ops:
  0.0 64.4 %copy-start = (bf16[1,8192,160]{1,2,0:T(8,128)(2,1)S(1)}, bf16[1,8192,160]{1,2,0:T(8,128)(2,1)}, u32[]{:S(2)}) copy-start(bf16[1,8192,160]{1,2,0:T(8,128)(2,1)} %param.16) | copy-start | bytes 7864324
  1.2 9.3 %copy-start.2 = (s32[1,1024]{1,0:T(1,128)S(1)}, s32[1,1024]{1,0:T(1,128)}, u32[]{:S(2)}) copy-start(s32[1,1024]{1,0:T(1,128)} %param.24) | copy-start | bytes 12292
  53.5 5.1 %copy-start.11 = (f32[256,64]{0,1:T(8,128)S(1)}, f32[256,64]{0,1:T(8,128)}, u32[]{:S(2)}) copy-start(f32[256,64]{0,1:T(8,128)} %constant.31.clone) | copy-start | bytes 196612
  53.5 5.1 %copy-start.12 = (f32[256,64]{0,1:T(8,128)S(1)}, f32[256,64]{0,1:T(8,128)}, u32[]{:S(2)}) copy-start(f32[256,64]{0,1:T(8,128)} %constant.32.clone) | copy-start | bytes 196612
  53.5 5.2 %copy-start.6 = (f32[256,64]{0,1:T(8,128)S(1)}, f32[256,64]{0,1:T(8,128)}, u32[]{:S(2)}) copy-start(f32[256,64]{0,1:T(8,128)} %constant.86.clone) | copy-start | bytes 196612
  53.5 5.2 %copy-start.7 = (f32[256,64]{0,1:T(8,128)S(1)}, f32[256,64]{0,1:T(8,128)}, u32[]{:S(2)}) copy-start(f32[256,64]{0,1:T(8,128)} %constant.87.clone) | copy-start | bytes 196612
  58.0 117.9 %collective-permute-start = (bf16[1,4,256,8,128]{4,3,2,1,0:T(8,128)(2,1)}, bf16[1,4,256,8,128]{4,3,2,1,0:T(8,128)(2,1)}, u32[]{:S(2)}, u32[]{:S(2)}) collective-permute-start(bf16[1,4,256,8,128]{4,3,2,1,0:T(8,128)(2,1)} %broadcast_select_fusion), channel_id=1, source_target_pairs={{0,1},{1,0},{2,3},{3,2},{4,5},{5,4},{6,7},{7,6},{8,9},{9,8},{10,11... | collective-permute-start | bytes 6291464 | tf_op jit(solution)/shard_map/ppermute | solution.py:16
  61.8 2.6 %copy-start.5 = (bf16[1,160,512]{2,1,0:T(8,128)(2,1)S(1)}, bf16[1,160,512]{2,1,0:T(8,128)(2,1)}, u32[]{:S(2)}) copy-start(bf16[1,160,512]{2,1,0:T(8,128)(2,1)} %param.17) | copy-start | bytes 491524
  113.7 4.5 %copy-start.10 = (bf16[1,4096]{1,0:T(2,128)(2,1)S(1)}, bf16[1,4096]{1,0:T(2,128)(2,1)}, u32[]{:S(2)}) copy-start(bf16[1,4096]{1,0:T(2,128)(2,1)} %param.22) | copy-start | bytes 24580
  126.0 2.6 %copy-start.4 = (bf16[1024,4,128]{2,1,0:T(4,128)(2,1)S(1)}, bf16[1024,4,128]{2,1,0:T(4,128)(2,1)}, u32[]{:S(2)}) copy-start(bf16[1024,4,128]{2,1,0:T(4,128)(2,1)} %select_convert_fusion) | copy-start | bytes 3145732
  133.2 30.0 %all-to-all-start.2 = ((f32[1,8,4]{2,0,1:T(1,128)}), f32[1,8,4]{2,0,1:T(1,128)S(1)}, u32[]{:S(2)}, u32[]{:S(2)}) async-start(f32[1,8,4]{2,0,1:T(1,128)} %bitcast.44), calls=%async_computation.2 | async-start | bytes 8192 | tf_op jit(solution)/shard_map/all_to_all | solution.py:223
  140.0 7.2 %copy-start.3 = (bf16[1,1024,512]{2,1,0:T(8,128)(2,1)S(1)}, bf16[1,1024,512]{2,1,0:T(8,128)(2,1)}, u32[]{:S(2)}) copy-start(bf16[1,1024,512]{2,1,0:T(8,128)(2,1)} %param.19) | copy-start | bytes 3145732
  146.5 1.0 copy-start.8
  146.5 1.3 copy-start.9
  163.1 12.5 %all-to-all-start.1 = ((f32[1,8,4]{2,0,1:T(1,128)}), f32[1,8,4]{2,0,1:T(1,128)S(1)}, u32[]{:S(2)}, u32[]{:S(2)}) async-start(f32[1,8,4]{2,0,1:T(1,128)} %bitcast.41), calls=%async_computation.1 | async-start | bytes 8192 | tf_op jit(solution)/shard_map/all_to_all | solution.py:220
  175.9 33.0 %copy-start.1 = (bf16[1,8192,160]{1,2,0:T(8,128)(2,1)S(1)}, bf16[1,8192,160]{1,2,0:T(8,128)(2,1)}, u32[]{:S(2)}) copy-start(bf16[1,8192,160]{1,2,0:T(8,128)(2,1)} %param.16) | copy-start | bytes 7864324
  181.4 9.9 %all-to-all-start = ((f32[1,32,128]{2,0,1:T(1,128)}), f32[1,32,128]{2,0,1:T(1,128)S(1)}, u32[]{:S(2)}, u32[]{:S(2)}) async-start(f32[1,32,128]{2,0,1:T(1,128)} %bitcast.39), calls=%async_computation | async-start | bytes 32768 | tf_op jit(solution)/shard_map/all_to_all | solution.py:226
where the time goes:
time: 210 us; the launch traced here: 209 us
  local copies, waits for them, and re-layouts  107 us (51%)
  other arithmetic  42.6 us (20%)
  blocking collectives  16.9 us (8%)
  starting transfers between devices  16.7 us (8%)
  waiting for transfers between devices  12.7 us (6%)
  matrix products  11.7 us (6%)
    reduce_min x1, other arithmetic, local(): low_keys = jnp.min(jnp.where(token_mask, paged_keys, jnp.inf), axis=2)  22.4 us
    gather x4, local copies, waits for them, and re-layouts, slot_pages(): picked = jnp.take_along_axis(padded, offsets, axis=-1)  18.3 us
    another operation x11, local copies, waits for them, and re-layouts  17.5 us
    all_gather x1, blocking collectives, local(): all_rows = lax.all_gather(rows_out, 'seq', axis=0, tiled=True)  16.9 us
    gather x1, local copies, waits for them, and re-layouts, local(): local_rows = value_store[request_idx, my_rank, :, my_heads, :]  12.5 us
    gather x1, local copies, waits for them, and re-layouts, local(): outgoing_rows = value_store[request_idx, other_rank, :, other_heads, :]  12.5 us
    gather x1, local copies, waits for them, and re-layouts, local(): paged_keys[request_idx, my_local, :, local_heads[None, :, None], :]  7.64 us
    all_to_all x1, starting transfers between devices, local(): lax.all_to_all(weight_sum.reshape(1, row_total), 'seq', split_axis=1, con...  6.83 us
  transfers between devices with their start and end apart: 4, of which 2 were waited for; matrix products, arithmetic and copies ran while one was open for 47% of the time, Pallas kernels for 0%

commit v1 on v0

--- a/solution.py
+++ b/solution.py
@@ -217,8 +217,14 @@
     row_total = requests * heads_here * group_size
     row_share = row_total // seq_count
     got_peak, got_sum, got_out = (
-        lax.all_to_all(
-            row_peak.reshape(1, row_total), "seq", split_axis=1, concat_axis=0, tiled=True
+        jnp.concatenate(
+            lax.all_to_all(
+                jnp.stack(jnp.split(row_peak.reshape(1, row_total), lax.axis_size("seq"), axis=1)),
+                "seq",
+                0,
+                0,
+            ),
+            axis=0,
         ),
         lax.all_to_all(
             weight_sum.reshape(1, row_total), "seq", split_axis=1, concat_axis=0, tiled=True

time: 210 us -> 216 us (1.029)
  local copies, waits for them, and re-layouts: 107 us -> 113 us
    all_to_all x1, waiting for transfers between devices: 6.31 us -> 0.01 us  [local(): lax.all_to_all(jnp.stack(jnp.split(row_peak.reshape(1, row_total), lax.ax...]
    all_to_all x1, waiting for transfers between devices: 0.01 us -> 6.31 us  [local(): lax.all_to_all(weight_sum.reshape(1, row_total), 'seq', split_axis=1, con...]
    unnamed x35 -> x42, local copies, waits for them, and re-layouts: 5.17 us -> 9.37 us
    another operation x11 -> x12, local copies, waits for them, and re-layouts: 17.5 us -> 19.2 us
  transfers between devices with their start and end apart: 4 -> 4, of which waited for: 2 -> 2; matrix products, arithmetic and copies ran while one was open for 47% -> 48% of each run, Pallas kernels for 0% -> 0%
where the time goes in v1:
time: 216 us; the launch traced here: 215 us
  local copies, waits for them, and re-layouts  113 us (52%)
  other arithmetic  42.8 us (20%)
  blocking collectives  16.9 us (8%)
  starting transfers between devices  16.7 us (8%)
  waiting for transfers between devices  12.7 us (6%)
  matrix products  11.7 us (5%)
    reduce_min x1, other arithmetic, local(): low_keys = jnp.min(jnp.where(token_mask, paged_keys, jnp.inf), axis=2)  23.4 us
    another operation x11, local copies, waits for them, and re-layouts  18.6 us
    gather x4, local copies, waits for them, and re-layouts, slot_pages(): picked = jnp.take_along_axis(padded, offsets, axis=-1)  18.3 us
    all_gather x1, blocking collectives, local(): all_rows = lax.all_gather(rows_out, 'seq', axis=0, tiled=True)  16.9 us
    gather x1, local copies, waits for them, and re-layouts, local(): local_rows = value_store[request_idx, my_rank, :, my_heads, :]  12.5 us
    gather x1, local copies, waits for them, and re-layouts, local(): outgoing_rows = value_store[request_idx, other_rank, :, other_heads, :]  12.5 us
    unnamed x42, local copies, waits for them, and re-layouts  9.37 us
    gather x1, local copies, waits for them, and re-layouts, local(): paged_keys[request_idx, my_local, :, local_heads[None, :, None], :]  7.64 us
  transfers between devices with their start and end apart: 4, of which 2 were waited for; matrix products, arithmetic and copies ran while one was open for 48% of the time, Pallas kernels for 0%

profile of v1, /device:TPU:0, one launch (start us, length us, event | category | flops | bytes accessed | tf_op | source)
XLA Modules:
  0.0 214.7 jit_solution(8264000936126237734)
XLA Ops:
  1.2 9.1 %gather_fusion.7 = s32[1024]{0:T(1024)S(1)} fusion(s32[4,1280]{1,0:T(4,128)S(1)} %get-tuple-element.43, s32[1024]{0:T(1024)S(1)} %bitcast.183), kind=kCustom, calls=%fused_computation.clone | custom fusion | bytes 16384 | tf_op jit(solution)/shard_map/jit(take_along_axis)/gather | solution.py:72
  11.9 9.1 %gather_fusion.8 = s32[1024]{0:T(1024)S(1)} fusion(s32[4,1280]{1,0:T(4,128)S(1)} %get-tuple-element.42, s32[1024]{0:T(1024)S(1)} %bitcast.184), kind=kCustom, calls=%fused_computation.1.clone | custom fusion | bytes 16384 | tf_op jit(solution)/shard_map/jit(take_along_axis)/gather | solution.py:72
  21.1 6.5 %gather_fusion.4 = s32[1024]{0:T(1024)S(1)} fusion(s32[1,1024]{1,0:T(1,128)S(1)} %copy-done.2, s32[1024]{0:T(1024)S(1)} %bitcast.178), kind=kCustom, calls=%fused_computation.6 | custom fusion | bytes 16384 | tf_op jit(solution)/shard_map/gather | solution.py:160
  27.7 6.5 %gather_fusion.5 = s32[1024]{0:T(1024)S(1)} fusion(s32[1,1024]{1,0:T(1,128)S(1)} %fusion.47, s32[1024]{0:T(1024)S(1)} %bitcast.179), kind=kCustom, calls=%fused_computation.7 | custom fusion | bytes 16384 | tf_op jit(solution)/shard_map/gather | solution.py:161
  34.2 6.5 %gather_fusion.2 = s32[1024]{0:T(1024)S(1)} fusion(s32[1,1024]{1,0:T(1,128)S(1)} %fusion.47, s32[1024]{0:T(1024)S(1)} %bitcast.176), kind=kCustom, calls=%fused_computation.4 | custom fusion | bytes 16384 | tf_op jit(solution)/shard_map/gather | solution.py:159
  41.0 12.5 %gather_fusion.6 = bf16[1024,8,128]{2,1,0:T(8,128)(2,1)} fusion(bf16[1,512,8,8,128]{4,2,3,1,0:T(8,128)(2,1)} %bitcast.193, s32[1024]{0:T(1024)S(1)} %bitcast.181), kind=kCustom, calls=%fused_computation.8 | custom fusion | bytes 4206592 | tf_op jit(solution)/shard_map/gather | solution.py:195
  53.5 4.5 %broadcast_select_fusion = bf16[1,4,256,8,128]{4,3,2,1,0:T(8,128)(2,1)} fusion(bf16[1,4,256,8,128]{4,3,2,1,0:T(8,128)(2,1)} %bitcast.189, pred[4,256]{1,0:T(4,128)(4,1)S(1)} %fusion.84), kind=kLoop, calls=%fused_computation.26 | loop fusion | flops 1048576 | bytes 4195328 | tf_op jit(solution)/shard_map/jit(_where)/select_n | solution.py:196
  66.7 5.9 %subtract_convert_fusion = (bf16[1,8192,4,64]{1,3,2,0:T(8,128)(2,1)}, bf16[1,8192,4,64]{1,3,2,0:T(8,128)(2,1)}) fusion(f32[1,8192,4,128]{1,3,2,0:T(8,128)S(1)} %convolution_bitcast_fusion, f32[8192,64]{0,1:T(8,128)} %bitcast.188, f32[8192,64]{0,1:T(8,128)} %bitcast.187), kind=kLoop, calls=%fused_computation.14 | loop fusion | flops 16777216 | bytes 29360128 | tf_op jit(solution)/shard_map/convert.3
  72.6 8.4 %copy.69 = bf16[1,8192,4,64]{3,1,2,0:T(8,128)(2,1)} copy(bf16[1,8192,4,64]{1,3,2,0:T(8,128)(2,1)} %get-tuple-element.22) | data formatting | bytes 8388608 | tf_op jit(solution)/shard_map/convert.2
  81.0 8.5 %copy.68 = bf16[1,8192,4,64]{3,1,2,0:T(8,128)(2,1)} copy(bf16[1,8192,4,64]{1,3,2,0:T(8,128)(2,1)} %get-tuple-element.21) | data formatting | bytes 8388608 | tf_op jit(solution)/shard_map/convert.3
  90.5 23.4 %select_reduce_fusion.1 = (bf16[1024,4,128]{2,1,0:T(4,128)(2,1)}, bf16[1024,4,128]{2,1,0:T(4,128)(2,1)}, bf16[1,1024,8,4,128]{4,2,3,1,0:T(8,128)(2,1)}) fusion(pred[1024,8]{1,0:T(8,128)(4,1)S(1)} %copy.66, bf16[1,1024,8,4,64]{4,2,1,3,0:T(8,128)(2,1)} %bitcast.185, bf16[1,1024,8,4,64]{4,2,1,3,0:T(8,128)(2,1)} %bitcast.186), kind=kLoop, calls=%fused_computation.12 | loop fusion | flops 32505856 | bytes 18882560 | tf_op jit(solution)/shard_map/reduce_min | solution.py:139
  114.0 7.6 %gather_fusion = bf16[1024,8,128]{2,1,0:T(8,128)(2,1)S(1)} fusion(bf16[1,1024,8,4,128]{4,2,3,1,0:T(8,128)(2,1)} %get-tuple-element.23, s32[1024]{0:T(1024)S(1)} %bitcast.180), kind=kCustom, calls=%fused_computation.2 | custom fusion | bytes 4206592 | tf_op jit(solution)/shard_map/gather | solution.py:164
  121.6 2.6 %fusion.40 = f32[4,256,8,8]{3,2,1,0:T(8,128)} fusion(bf16[4,256,8,128]{3,2,1,0:T(8,128)(2,1)S(1)} %bitcast.192, bf16[4096]{0:T(1024)(128)(2,1)S(1)} %reduce.21), kind=kOutput, calls=%fused_computation.91 | convolution fusion | flops 16777216 | bytes 2367488 | tf_op jit(solution)/shard_map/rhgd,rhcpd->rhgcp/dot_general | solution.py:166
  124.2 3.0 %copy.73 = f32[4,256,8,8]{1,2,3,0:T(8,128)S(1)} copy(f32[4,256,8,8]{3,2,1,0:T(8,128)} %fusion.40) | data formatting | bytes 524288 | tf_op jit(solution)/shard_map/rhgd,rhcpd->rhgcp/dot_general | solution.py:166
  128.0 3.8 %select_convert_fusion = bf16[1024,4,128]{2,1,0:T(4,128)(2,1)S(1)} fusion(bf16[1024,4,128]{2,1,0:T(4,128)(2,1)S(1)} %copy-done.4, bf16[1024,4,128]{2,1,0:T(4,128)(2,1)S(1)} %copy-done.3, pred[1024]{0:T(1024)(128)(4,1)S(1)} %fusion.29), kind=kLoop, calls=%fused_computation.22 | loop fusion | flops 3145728 | bytes 3146752 | tf_op jit(solution)/shard_map/convert_element_type | solution.py:145
  137.4 6.8 %all-to-all-start.1 = ((f32[8,1,4]{2,1,0:T(1,128)}), f32[8,1,4]{2,1,0:T(1,128)S(1)}, u32[]{:S(2)}, u32[]{:S(2)}) async-start(f32[8,1,4]{2,1,0:T(1,128)} %constant_dynamic-update-slice_fusion), calls=%async_computation.1 | async-start | bytes 8192 | tf_op jit(solution)/shard_map/all_to_all | solution.py:221
  144.2 6.4 %gather_fusion.1 = s32[1024]{0:T(1024)S(1)} fusion(s32[1,1024]{1,0:T(1,128)S(1)} %copy-done.2, s32[1024]{0:T(1024)S(1)} %bitcast.177), kind=kCustom, calls=%fused_computation.3 | custom fusion | bytes 16384 | tf_op jit(solution)/shard_map/gather | solution.py:158
  154.4 12.5 %gather_fusion.3 = bf16[1024,8,128]{2,1,0:T(8,128)(2,1)} fusion(bf16[1,512,8,8,128]{4,2,3,1,0:T(8,128)(2,1)} %bitcast.194, s32[1024]{0:T(1024)S(1)} %bitcast.182), kind=kCustom, calls=%fused_computation.5 | custom fusion | bytes 4206592 | tf_op jit(solution)/shard_map/gather | solution.py:194
  169.0 6.0 %all-to-all-start.2 = ((f32[1,8,4]{2,0,1:T(1,128)}), f32[1,8,4]{2,0,1:T(1,128)S(1)}, u32[]{:S(2)}, u32[]{:S(2)}) async-start(f32[1,8,4]{2,0,1:T(1,128)} %bitcast.51), calls=%async_computation.2 | async-start | bytes 8192 | tf_op jit(solution)/shard_map/all_to_all | solution.py:229
  175.1 6.3 %all-to-all-done.2 = f32[1,8,4]{2,0,1:T(1,128)S(1)} async-done(((f32[1,8,4]{2,0,1:T(1,128)}), f32[1,8,4]{2,0,1:T(1,128)S(1)}, u32[]{:S(2)}, u32[]{:S(2)}) %all-to-all-start.2) | async-done | bytes 160 | tf_op jit(solution)/shard_map/all_to_all | solution.py:229
  181.7 5.5 %fusion.12 = f32[4,8,128]{2,1,0:T(8,128)} fusion(f32[4,8,128]{2,1,0:T(8,128)S(1)} %fusion.15, bf16[4,8,256,8]{3,1,2,0:T(8,128)(2,1)} %copy.75, bf16[1,4,256,8,128]{4,3,2,1,0:T(8,128)(2,1)} %bitcast.195, bf16[1,4,256,8,128]{4,3,2,1,0:T(8,128)(2,1)} %collective-permute-done, pred[4,256]{1,0:T(4,128)(4,1)S(1)} %reshape.1020), kind=kOutput, calls=%fused_computation.33 | convolution fusion | flops 17829888 | bytes 4359168 | tf_op jit(solution)/shard_map/rhgcp,rhcpd->rhgd/dot_general | solution.py:199
  187.2 3.3 %all-to-all-start = ((f32[1,32,128]{2,0,1:T(1,128)}), f32[1,32,128]{2,0,1:T(1,128)S(1)}, u32[]{:S(2)}, u32[]{:S(2)}) async-start(f32[1,32,128]{2,0,1:T(1,128)} %bitcast.39), calls=%async_computation | async-start | bytes 32768 | tf_op jit(solution)/shard_map/all_to_all | solution.py:232
  190.7 6.3 %all-to-all-done = f32[1,32,128]{2,0,1:T(1,128)S(1)} async-done(((f32[1,32,128]{2,0,1:T(1,128)}), f32[1,32,128]{2,0,1:T(1,128)S(1)}, u32[]{:S(2)}, u32[]{:S(2)}) %all-to-all-start) | async-done | bytes 16416 | tf_op jit(solution)/shard_map/all_to_all | solution.py:232
  197.2 16.9 %all-gather = bf16[8,4,128]{2,1,0:T(4,128)(2,1)S(1)} all-gather(bf16[1,4,128]{2,1,0:T(4,128)(2,1)S(1)} %fusion.88), channel_id=1, replica_groups=mesh['grp'=2,'seq'=8,'pool'=2] {'seq'}, dimensions={0}, use_global_device_ids=true | all-gather | bytes 9216 | tf_op jit(solution)/shard_map/all_gather | solution.py:248
  (126 shorter events, 25.7 us)
Async XLA Ops:
  0.0 64.4 %copy-start = (bf16[1,8192,160]{1,2,0:T(8,128)(2,1)S(1)}, bf16[1,8192,160]{1,2,0:T(8,128)(2,1)}, u32[]{:S(2)}) copy-start(bf16[1,8192,160]{1,2,0:T(8,128)(2,1)} %param.16) | copy-start | bytes 7864324
  1.2 9.3 %copy-start.2 = (s32[1,1024]{1,0:T(1,128)S(1)}, s32[1,1024]{1,0:T(1,128)}, u32[]{:S(2)}) copy-start(s32[1,1024]{1,0:T(1,128)} %param.24) | copy-start | bytes 12292
  53.5 5.1 %copy-start.11 = (f32[256,64]{0,1:T(8,128)S(1)}, f32[256,64]{0,1:T(8,128)}, u32[]{:S(2)}) copy-start(f32[256,64]{0,1:T(8,128)} %constant.31.clone) | copy-start | bytes 196612
  53.5 5.1 %copy-start.12 = (f32[256,64]{0,1:T(8,128)S(1)}, f32[256,64]{0,1:T(8,128)}, u32[]{:S(2)}) copy-start(f32[256,64]{0,1:T(8,128)} %constant.32.clone) | copy-start | bytes 196612
  53.5 5.2 %copy-start.6 = (f32[256,64]{0,1:T(8,128)S(1)}, f32[256,64]{0,1:T(8,128)}, u32[]{:S(2)}) copy-start(f32[256,64]{0,1:T(8,128)} %constant.86.clone) | copy-start | bytes 196612
  53.5 5.2 %copy-start.7 = (f32[256,64]{0,1:T(8,128)S(1)}, f32[256,64]{0,1:T(8,128)}, u32[]{:S(2)}) copy-start(f32[256,64]{0,1:T(8,128)} %constant.87.clone) | copy-start | bytes 196612
  58.0 123.7 %collective-permute-start = (bf16[1,4,256,8,128]{4,3,2,1,0:T(8,128)(2,1)}, bf16[1,4,256,8,128]{4,3,2,1,0:T(8,128)(2,1)}, u32[]{:S(2)}, u32[]{:S(2)}) collective-permute-start(bf16[1,4,256,8,128]{4,3,2,1,0:T(8,128)(2,1)} %broadcast_select_fusion), channel_id=1, source_target_pairs={{0,1},{1,0},{2,3},{3,2},{4,5},{5,4},{6,7},{7,6},{8,9},{9,8},{10,11... | collective-permute-start | bytes 6291464 | tf_op jit(solution)/shard_map/ppermute | solution.py:16
  61.8 2.6 %copy-start.5 = (bf16[1,160,512]{2,1,0:T(8,128)(2,1)S(1)}, bf16[1,160,512]{2,1,0:T(8,128)(2,1)}, u32[]{:S(2)}) copy-start(bf16[1,160,512]{2,1,0:T(8,128)(2,1)} %param.17) | copy-start | bytes 491524
  81.0 9.5 %copy-start.10 = (bf16[1,4096]{1,0:T(2,128)(2,1)S(1)}, bf16[1,4096]{1,0:T(2,128)(2,1)}, u32[]{:S(2)}) copy-start(bf16[1,4096]{1,0:T(2,128)(2,1)} %param.22) | copy-start | bytes 24580
  124.2 3.8 %copy-start.3 = (bf16[1024,4,128]{2,1,0:T(4,128)(2,1)S(1)}, bf16[1024,4,128]{2,1,0:T(4,128)(2,1)}, u32[]{:S(2)}) copy-start(bf16[1024,4,128]{2,1,0:T(4,128)(2,1)} %get-tuple-element.6) | copy-start | bytes 3145732
  124.2 3.8 %copy-start.4 = (bf16[1024,4,128]{2,1,0:T(4,128)(2,1)S(1)}, bf16[1024,4,128]{2,1,0:T(4,128)(2,1)}, u32[]{:S(2)}) copy-start(bf16[1024,4,128]{2,1,0:T(4,128)(2,1)} %get-tuple-element.7) | copy-start | bytes 3145732
  137.4 31.6 %all-to-all-start.1 = ((f32[8,1,4]{2,1,0:T(1,128)}), f32[8,1,4]{2,1,0:T(1,128)S(1)}, u32[]{:S(2)}, u32[]{:S(2)}) async-start(f32[8,1,4]{2,1,0:T(1,128)} %constant_dynamic-update-slice_fusion), calls=%async_computation.1 | async-start | bytes 8192 | tf_op jit(solution)/shard_map/all_to_all | solution.py:221
  154.4 12.6 %copy-start.8 = (bf16[1,64,512]{2,1,0:T(8,128)(2,1)S(1)}, bf16[1,64,512]{2,1,0:T(8,128)(2,1)}, u32[]{:S(2)}) copy-start(bf16[1,64,512]{2,1,0:T(8,128)(2,1)} %param.20) | copy-start | bytes 196612
  154.4 12.9 %copy-start.9 = (bf16[1,64,512]{2,1,0:T(8,128)(2,1)S(1)}, bf16[1,64,512]{2,1,0:T(8,128)(2,1)}, u32[]{:S(2)}) copy-start(bf16[1,64,512]{2,1,0:T(8,128)(2,1)} %param.21) | copy-start | bytes 196612
  169.0 12.4 %all-to-all-start.2 = ((f32[1,8,4]{2,0,1:T(1,128)}), f32[1,8,4]{2,0,1:T(1,128)S(1)}, u32[]{:S(2)}, u32[]{:S(2)}) async-start(f32[1,8,4]{2,0,1:T(1,128)} %bitcast.51), calls=%async_computation.2 | async-start | bytes 8192 | tf_op jit(solution)/shard_map/all_to_all | solution.py:229
  181.7 33.0 %copy-start.1 = (bf16[1,8192,160]{1,2,0:T(8,128)(2,1)S(1)}, bf16[1,8192,160]{1,2,0:T(8,128)(2,1)}, u32[]{:S(2)}) copy-start(bf16[1,8192,160]{1,2,0:T(8,128)(2,1)} %param.16) | copy-start | bytes 7864324
  187.2 9.9 %all-to-all-start = ((f32[1,32,128]{2,0,1:T(1,128)}), f32[1,32,128]{2,0,1:T(1,128)S(1)}, u32[]{:S(2)}, u32[]{:S(2)}) async-start(f32[1,32,128]{2,0,1:T(1,128)} %bitcast.39), calls=%async_computation | async-start | bytes 32768 | tf_op jit(solution)/shard_map/all_to_all | solution.py:232
